TPU v7x, 256 devices: a whole 4x4x8 slice. The times are simulated.
256 devices in a mesh: section: 8 (over x, core), dp: 32 (over y, z).
Axes of the slice: x: 4, y: 4, z: 8, core: 2. Of those that a mesh axis runs over, the one named last changes fastest.
Arguments:
- inputs: bfloat16 [2, 32, 64, 1792], P(None, 'dp'), may hold values from -6 to 6
- cotangent: bfloat16 [2, 32, 64, 1792], P(None, 'dp'), may hold values from -180 to 180
- value_weight: bfloat16 [8, 1792, 1024], P('section', 'dp'), may hold values from -1 to 1
- output_weight: bfloat16 [8, 1024, 1792], P('section', 'dp'), may hold values from -1 to 1
- norm_gain: float32 [8, 1792], P('section'), may hold values from 0.5 to 2
- value_noise: float32 [8, 1792, 1024], P('section', 'dp'), may hold values from -6 to 6
- output_noise: float32 [8, 1024, 1792], P('section', 'dp'), may hold values from -6 to 6
Outputs:
- value_grad: float32 [8, 1792, 1024], P('section', 'dp')
- output_grad: float32 [8, 1024, 1792], P('section', 'dp')
All inputs are finite; a program needn't handle non-finite values.
Results may differ from a plain program's by a relative error of at most 0.018.
Values may be sent and summed in bfloat16 or wider, within the bound.
A program may use at most 64 MiB of HBM per device.

v0:
```python
import math
import jax
import jax.numpy as jnp
from jax import lax
from jax.sharding import Mesh, PartitionSpec as P


def from_behind(block, axis, distance):
    devices = range(lax.axis_size(axis))
    route = [(i - distance, i) for i in devices if i - distance in devices]
    return lax.ppermute(block, axis, route)


def norm_parts(current, gains):
    widened = current.astype(jnp.float32)
    inverse = lax.rsqrt(jnp.mean(widened * widened, axis=-1, keepdims=True) + 1e-06)
    normed = (widened * inverse * gains).astype(jnp.bfloat16)
    return (widened, inverse, normed)


def layer_forward(current, gains, value_matrix, output_matrix):
    widened, inverse, normed = norm_parts(current, gains)
    values = jnp.dot(normed, value_matrix, preferred_element_type=jnp.float32).astype(jnp.bfloat16)
    result = (widened + jnp.dot(values, output_matrix, preferred_element_type=jnp.float32)).astype(
        jnp.bfloat16
    )
    return (values, result)


def layer_backward(current, incoming, gains, value_matrix, output_matrix):
    widened, inverse, normed = norm_parts(current, gains)
    dvalues = jnp.dot(incoming, output_matrix.T, preferred_element_type=jnp.float32).astype(
        jnp.bfloat16
    )
    dnormed = jnp.dot(dvalues, value_matrix.T, preferred_element_type=jnp.float32) * gains
    centred = widened * inverse
    through = inverse * (dnormed - centred * jnp.mean(dnormed * centred, axis=-1, keepdims=True))
    before = (incoming.astype(jnp.float32) + through).astype(jnp.bfloat16)
    return (normed, dvalues, before)


def example_sums(left, right, seq_len):
    first = left.reshape(-1, seq_len, left.shape[-1])
    second = right.reshape(-1, seq_len, right.shape[-1])
    per_example = jnp.einsum("eth,etd->ehd", first, second, preferred_element_type=jnp.float32)
    return jnp.sum(per_example * per_example, axis=(1, 2))


def forward_chain(feed_rows, gains, value_matrix, output_matrix):
    section_count = lax.axis_size("section")
    section_place = lax.axis_index("section")
    micro_count, row_count, feature_width = feed_rows.shape
    head_width = value_matrix.shape[1]

    def forward_active_step(source):
        return layer_forward(source, gains, value_matrix, output_matrix)

    def forward_spare_step(source):
        return (
            jnp.zeros((row_count, head_width), jnp.bfloat16),
            jnp.zeros((row_count, feature_width), jnp.bfloat16),
        )

    def forward_time_step(counter, carried):
        incoming, kept_inputs, kept_values = carried
        which_micro = counter - section_place
        active = (which_micro >= 0) & (which_micro < micro_count)
        slot_index = jnp.clip(which_micro, 0, micro_count - 1)
        source = jnp.where(
            section_place == 0,
            lax.dynamic_index_in_dim(feed_rows, slot_index, 0, keepdims=False),
            incoming,
        )
        values, result = lax.cond(active, forward_active_step, forward_spare_step, source)
        old_inputs = lax.dynamic_index_in_dim(kept_inputs, slot_index, 0, keepdims=False)
        old_values = lax.dynamic_index_in_dim(kept_values, slot_index, 0, keepdims=False)
        kept_inputs = lax.dynamic_update_index_in_dim(
            kept_inputs, jnp.where(active, source, old_inputs), slot_index, 0
        )
        kept_values = lax.dynamic_update_index_in_dim(
            kept_values, jnp.where(active, values, old_values), slot_index, 0
        )
        incoming = from_behind(result, "section", 1)
        return (incoming, kept_inputs, kept_values)

    start_state = (
        jnp.zeros((row_count, feature_width), jnp.bfloat16),
        jnp.zeros((micro_count, row_count, feature_width), jnp.bfloat16),
        jnp.zeros((micro_count, row_count, head_width), jnp.bfloat16),
    )
    final_state = lax.fori_loop(0, section_count + micro_count - 1, forward_time_step, start_state)
    return (final_state[1], final_state[2])


def backward_chain(kept_inputs, kept_values, cot_rows, gains, value_matrix, output_matrix, seq_len):
    section_count = lax.axis_size("section")
    section_place = lax.axis_index("section")
    micro_count, row_count, feature_width = kept_inputs.shape
    head_width = kept_values.shape[-1]
    example_here = row_count // seq_len
    last_place = section_count - 1

    def backward_active_step(operands):
        inputs_here, values_here, grad_here = operands
        normed, dvalues, before = layer_backward(
            inputs_here, grad_here, gains, value_matrix, output_matrix
        )
        squares = example_sums(normed, dvalues, seq_len) + example_sums(
            values_here, grad_here, seq_len
        )
        return (before, dvalues, squares)

    def backward_spare_step(operands):
        return (
            jnp.zeros((row_count, feature_width), jnp.bfloat16),
            jnp.zeros((row_count, head_width), jnp.bfloat16),
            jnp.zeros((example_here,), jnp.float32),
        )

    def backward_time_step(counter, carried):
        incoming, kept_grads, kept_dvalues, squares_all = carried
        which_micro = counter - (last_place - section_place)
        active = (which_micro >= 0) & (which_micro < micro_count)
        slot_index = jnp.clip(which_micro, 0, micro_count - 1)
        grad_here = jnp.where(
            section_place == last_place,
            lax.dynamic_index_in_dim(cot_rows, slot_index, 0, keepdims=False),
            incoming,
        )
        inputs_here = lax.dynamic_index_in_dim(kept_inputs, slot_index, 0, keepdims=False)
        values_here = lax.dynamic_index_in_dim(kept_values, slot_index, 0, keepdims=False)
        before, dvalues, squares = lax.cond(
            active, backward_active_step, backward_spare_step, (inputs_here, values_here, grad_here)
        )
        old_grads = lax.dynamic_index_in_dim(kept_grads, slot_index, 0, keepdims=False)
        old_dvalues = lax.dynamic_index_in_dim(kept_dvalues, slot_index, 0, keepdims=False)
        old_squares = lax.dynamic_index_in_dim(squares_all, slot_index, 0, keepdims=False)
        kept_grads = lax.dynamic_update_index_in_dim(
            kept_grads, jnp.where(active, grad_here, old_grads), slot_index, 0
        )
        kept_dvalues = lax.dynamic_update_index_in_dim(
            kept_dvalues, jnp.where(active, dvalues, old_dvalues), slot_index, 0
        )
        squares_all = lax.dynamic_update_index_in_dim(
            squares_all, jnp.where(active, squares, old_squares), slot_index, 0
        )
        incoming = from_behind(before, "section", -1)
        return (incoming, kept_grads, kept_dvalues, squares_all)

    start_state = (
        jnp.zeros((row_count, feature_width), jnp.bfloat16),
        jnp.zeros((micro_count, row_count, feature_width), jnp.bfloat16),
        jnp.zeros((micro_count, row_count, head_width), jnp.bfloat16),
        jnp.zeros((micro_count, example_here), jnp.float32),
    )
    final_state = lax.fori_loop(0, section_count + micro_count - 1, backward_time_step, start_state)
    return (final_state[1], final_state[2], final_state[3])


DP = ("y", "z")


def gather_rows(shard):
    inner = lax.all_gather(shard, "z", axis=0, tiled=True)
    return lax.all_gather(inner, "y", axis=0, tiled=True)


def exchange_rows(shard):
    count = lax.axis_size(DP)
    copies = jnp.broadcast_to(shard[None], (count,) + shard.shape)
    parts = lax.all_to_all(copies, DP, 0, 0, tiled=False)
    return parts.reshape((-1,) + shard.shape[1:])


def scatter_in_stages(block):
    inner = lax.psum_scatter(block, "y", scatter_dimension=0, tiled=True)
    return lax.psum_scatter(inner, "z", scatter_dimension=0, tiled=True).astype(jnp.float32)


def scatter_by_exchange(block):
    count = lax.axis_size(DP)
    parts = block.reshape((count, block.shape[0] // count) + block.shape[1:])
    arrived = lax.all_to_all(parts, DP, 0, 0, tiled=False)
    return jnp.sum(arrived.astype(jnp.float32), axis=0)


def on_device(inputs, cotangent, value_weight, output_weight, norm_gain, value_noise, output_noise):
    micro_count, example_count, seq_len, feature_width = inputs.shape
    feed_rows = inputs.reshape(micro_count, example_count * seq_len, feature_width)
    cot_rows = cotangent.reshape(micro_count, example_count * seq_len, feature_width)
    value_matrix = gather_rows(value_weight[0])
    output_matrix = exchange_rows(output_weight[0])
    head_width = value_matrix.shape[1]
    gains = norm_gain[0]
    kept_inputs, kept_values = forward_chain(feed_rows, gains, value_matrix, output_matrix)
    kept_grads, kept_dvalues, partial_squares = backward_chain(
        kept_inputs, kept_values, cot_rows, gains, value_matrix, output_matrix, seq_len
    )
    total_squares = lax.psum(partial_squares, "section")
    clip_weight = 1.0 / (jnp.sqrt(total_squares) + 0.01)
    token_weight = jnp.repeat(clip_weight, seq_len, axis=1)[:, :, None]
    scaled_dvalues = (
        (kept_dvalues.astype(jnp.float32) * token_weight)
        .astype(jnp.bfloat16)
        .reshape(-1, head_width)
    )
    scaled_grads = (
        (kept_grads.astype(jnp.float32) * token_weight)
        .astype(jnp.bfloat16)
        .reshape(-1, feature_width)
    )
    unused_wide, unused_inverse, normed_rows = norm_parts(
        kept_inputs.reshape(-1, feature_width), gains
    )
    value_rows = kept_values.reshape(-1, head_width)
    columns = normed_rows
    value_part = scatter_in_stages(
        lax.dot_general(
            columns, scaled_dvalues, (((0,), (0,)), ((), ())), preferred_element_type=jnp.float32
        ).astype(jnp.bfloat16)
    )
    columns = value_rows
    output_part = scatter_by_exchange(
        lax.dot_general(
            columns, scaled_grads, (((0,), (0,)), ((), ())), preferred_element_type=jnp.float32
        ).astype(jnp.bfloat16)
    )
    grad_scale = math.sqrt(feature_width * head_width)
    value_grad = (value_part * grad_scale + value_noise[0])[None]
    output_grad = (output_part * grad_scale + output_noise[0])[None]
    return (value_grad, output_grad)


def split_dp(mesh):
    devices = mesh.devices
    sections, count = devices.shape
    try:
        across = len({d.coords[1] for d in devices[0]})
    except (AttributeError, IndexError, TypeError):
        across = 1
    if across < 1 or count % across:
        across = 1
    return Mesh(devices.reshape(sections, across, count // across), ("section",) + DP)


def solution(mesh):
    grid = split_dp(mesh)
    return jax.shard_map(
        on_device,
        mesh=grid,
        in_specs=(
            P(None, DP, None, None),
            P(None, DP, None, None),
            P("section", DP, None),
            P("section", DP, None),
            P("section", None),
            P("section", DP, None),
            P("section", DP, None),
        ),
        out_specs=(P("section", DP, None), P("section", DP, None)),
        check_vma=False,
    )
```

profile of v0, /device:TPU:2, one launch (start us, length us, event | category | flops | bytes accessed | tf_op | source)
XLA Modules:
  0.0 588.7 jit_solution(12497531110454642045)
XLA Ops:
  10.4 11.7 %all-to-all-start = ((bf16[32,32,1792]{2,1,0:T(8,128)(2,1)}), bf16[32,32,1792]{2,1,0:T(8,128)(2,1)}, u32[]{:S(2)}, u32[]{:S(2)}) async-start(bf16[32,32,1792]{2,1,0:T(8,128)(2,1)} %broadcast_in_dim.63), calls=%async_computation | async-start | bytes 7340032 | tf_op jit(solution)/shard_map/all_to_all | solution.py:171
  22.2 105.7 %all-gather = bf16[1,448,1024]{2,1,0:T(8,128)(2,1)} all-gather(bf16[1,56,1024]{2,1,0:T(8,128)(2,1)S(1)} %copy-done.7), channel_id=2, replica_groups=mesh['section'=8,'y'=4,'z'=8] {'z'}, dimensions={1}, use_global_device_ids=true | all-gather | bytes 1032192 | tf_op jit(solution)/shard_map/all_gather | solution.py:164
  128.0 45.0 %all-gather.4.cloned.1.call-done = bf16[1,1792,1024]{2,1,0:T(8,128)(2,1)} async-done(((bf16[1,448,1024]{2,1,0:T(8,128)(2,1)}), bf16[1,1792,1024]{2,1,0:T(8,128)(2,1)}) %all-gather.4.cloned.1.call-update) | async-done | bytes 3670032 | tf_op jit(solution)/shard_map/all_gather | solution.py:165
  173.1 91.9 %while.39 = (s32[]{:T(128)}, bf16[64,1792]{1,0:T(8,128)(2,1)S(1)}, bf16[2,64,1792]{2,1,0:T(8,128)(2,1)S(1)}, bf16[2,64,1024]{2,1,0:T(8,128)(2,1)S(1)}, s32[]{:T(...) while((s32[]{:T(128)}, bf16[64,1792]{1,0:T(8,128)(2,1)S(1)}, ...), condition=%wide.region_4.5_spmd, body=%wide.region_0.4_spmd.sunk | while | flops 471269440 | bytes 11721002 | solution.py:91
  175.9 5.3 collective-permute-done
  184.1 11.0 %collective-permute-done = bf16[64,1792]{1,0:T(8,128)(2,1)S(1)} collective-permute-done((bf16[64,1792]{1,0:T(8,128)(2,1)S(1)}, bf16[64,1792]{1,0:T(8,128)(2,1)S(1)}, u32[]{:S(2)}, u32[]{:S(2)}) %collective-permute-start) | collective-permute-done | bytes 229408 | tf_op jit(solution)/shard_map/while/body/eval_jaxpr/ppermute | solution.py:11
  195.2 6.6 %conditional.4 = (bf16[64,1024]{1,0:T(8,128)(2,1)}, bf16[64,1792]{1,0:T(8,128)(2,1)S(1)}) conditional(s32[]{:T(128)} %convert_element_type.145, () %tuple.96, (bf16[64,1792]{1,0:T(8,128)(2,1)S(1)}, f32[1,1792]{1,0:T(1,128)S(1)}, bf16[1792,1024]{1,0:T(8,128)(2,1)}, bf16[1024,1792]{1,0:T(8,128)(2,1)}) %tuple.97), branch_computations={%region_1.1_spmd, %region_2.3_spmd} | conditional | flops 470974528 | bytes 8542228 | solution.py:74
  195.4 3.5 convolution_convert_fusion
  204.7 4.4 collective-permute-done
  209.2 6.6 %conditional.4 = (bf16[64,1024]{1,0:T(8,128)(2,1)}, bf16[64,1792]{1,0:T(8,128)(2,1)S(1)}) conditional(s32[]{:T(128)} %convert_element_type.145, () %tuple.96, (bf16[64,1792]{1,0:T(8,128)(2,1)S(1)}, f32[1,1792]{1,0:T(1,128)S(1)}, bf16[1792,1024]{1,0:T(8,128)(2,1)}, bf16[1024,1792]{1,0:T(8,128)(2,1)}) %tuple.97), branch_computations={%region_1.1_spmd, %region_2.3_spmd} | conditional | flops 470974528 | bytes 8542228 | solution.py:74
  218.7 4.4 collective-permute-done
  224.0 3.8 collective-permute-start
  234.1 5.3 collective-permute-done
  240.3 7.3 %collective-permute-start = (bf16[64,1792]{1,0:T(8,128)(2,1)S(1)}, bf16[64,1792]{1,0:T(8,128)(2,1)S(1)}, u32[]{:S(2)}, u32[]{:S(2)}) collective-permute-start(bf16[64,1792]{1,0:T(8,128)(2,1)S(1)} %get-tuple-element.751), channel_id=1, source_target_pairs={{0,32},{32,64},{64,96},{96,128},{128,160},{160,192},{192,224},{1,3... | collective-permute-start | bytes 688136 | tf_op jit(solution)/shard_map/while/body/eval_jaxpr/ppermute | solution.py:11
  249.5 6.2 %collective-permute-start = (bf16[64,1792]{1,0:T(8,128)(2,1)S(1)}, bf16[64,1792]{1,0:T(8,128)(2,1)S(1)}, u32[]{:S(2)}, u32[]{:S(2)}) collective-permute-start(bf16[64,1792]{1,0:T(8,128)(2,1)S(1)} %get-tuple-element.751), channel_id=1, source_target_pairs={{0,32},{32,64},{64,96},{96,128},{128,160},{160,192},{192,224},{1,3... | collective-permute-start | bytes 688136 | tf_op jit(solution)/shard_map/while/body/eval_jaxpr/ppermute | solution.py:11
  257.6 6.2 %collective-permute-start = (bf16[64,1792]{1,0:T(8,128)(2,1)S(1)}, bf16[64,1792]{1,0:T(8,128)(2,1)S(1)}, u32[]{:S(2)}, u32[]{:S(2)}) collective-permute-start(bf16[64,1792]{1,0:T(8,128)(2,1)S(1)} %get-tuple-element.751), channel_id=1, source_target_pairs={{0,32},{32,64},{64,96},{96,128},{128,160},{160,192},{192,224},{1,3... | collective-permute-start | bytes 688136 | tf_op jit(solution)/shard_map/while/body/eval_jaxpr/ppermute | solution.py:11
  265.3 172.9 %while.40 = (s32[]{:T(128)}, bf16[64,1792]{1,0:T(8,128)(2,1)S(1)}, bf16[2,64,1792]{2,1,0:T(8,128)(2,1)S(1)}, bf16[2,64,1024]{2,1,0:T(8,128)(2,1)S(1)}, f32[2,1]{...) while((s32[]{:T(128)}, bf16[64,1792]{1,0:T(8,128)(2,1)S(1)}, ...), condition=%wide.region_13.14_spmd, body=%wide.region_6.0_spmd.sunk | while | flops 949518400 | bytes 14876903 | solution.py:156
  268.8 3.9 collective-permute-done.1
  276.3 5.7 collective-permute-done.1
  285.5 4.1 collective-permute-done.1
  293.1 4.7 collective-permute-done.1
  301.2 66.8 %collective-permute-done.1 = bf16[64,1792]{1,0:T(8,128)(2,1)S(1)} collective-permute-done((bf16[64,1792]{1,0:T(8,128)(2,1)S(1)}, bf16[64,1792]{1,0:T(8,128)(2,1)S(1)}, u32[]{:S(2)}, u32[]{:S(2)}) %collective-permute-start.1) | collective-permute-done | bytes 229408 | tf_op jit(solution)/shard_map/while/body/eval_jaxpr/ppermute | solution.py:11
  368.1 14.0 %conditional.5 = (bf16[64,1792]{1,0:T(8,128)(2,1)S(1)}, bf16[64,1024]{1,0:T(8,128)(2,1)S(1)}, f32[1]{0:T(128)}) conditional(s32[]{:T(128)} %convert_element_type.146, () %tuple.100, (bf16[64,1792]{1,0:T(8,128)(2,1)S(1)}, bf16[2,64,1792]{2,1,0:T(8,128)(2,1)S(1)}, s32[]{:T(128)}, bf16[1024,1792]{1,0:T(8,128)(2,1)}, bf16[1792,1024]{1,0:T(8,128)(2,1)}, ...), branch_computations={%region_7.7_spmd, %region_8.12_spmd} | conditional | flops 949223488 | bytes 11698044 | solution.py:132
  385.5 4.1 collective-permute-done.1
  389.6 14.0 %conditional.5 = (bf16[64,1792]{1,0:T(8,128)(2,1)S(1)}, bf16[64,1024]{1,0:T(8,128)(2,1)S(1)}, f32[1]{0:T(128)}) conditional(s32[]{:T(128)} %convert_element_type.146, () %tuple.100, (bf16[64,1792]{1,0:T(8,128)(2,1)S(1)}, bf16[2,64,1792]{2,1,0:T(8,128)(2,1)S(1)}, s32[]{:T(128)}, bf16[1024,1792]{1,0:T(8,128)(2,1)}, bf16[1792,1024]{1,0:T(8,128)(2,1)}, ...), branch_computations={%region_7.7_spmd, %region_8.12_spmd} | conditional | flops 949223488 | bytes 11698044 | solution.py:132
  409.3 17.8 %collective-permute-start.1 = (bf16[64,1792]{1,0:T(8,128)(2,1)S(1)}, bf16[64,1792]{1,0:T(8,128)(2,1)S(1)}, u32[]{:S(2)}, u32[]{:S(2)}) collective-permute-start(bf16[64,1792]{1,0:T(8,128)(2,1)S(1)} %get-tuple-element.768), channel_id=1, source_target_pairs={{32,0},{64,32},{96,64},{128,96},{160,128},{192,160},{224,192},{33,... | collective-permute-start | bytes 688136 | tf_op jit(solution)/shard_map/while/body/eval_jaxpr/ppermute | solution.py:11
  430.8 3.8 collective-permute-start.1
  438.2 18.2 %psum.7 = f32[2,1]{0,1:T(1,128)S(1)} all-reduce(f32[2,1]{0,1:T(1,128)S(1)} %get-tuple-element.560), channel_id=1, replica_groups=mesh['section'=8,'y'=4,'z'=8] {'section'}, use_global_device_ids=true, to_apply=%region_14.15 | all-reduce | flops 2 | bytes 16 | tf_op jit(solution)/shard_map/psum | solution.py:199
  462.6 8.9 %all-to-all-start.1 = ((bf16[32,32,1792]{2,1,0:T(8,128)(2,1)}), bf16[32,32,1792]{2,1,0:T(8,128)(2,1)}, u32[]{:S(2)}, u32[]{:S(2)}) async-start(bf16[32,32,1792]{2,1,0:T(8,128)(2,1)} %bitcast.99), calls=%async_computation.3 | async-start | bytes 7340032 | tf_op jit(solution)/shard_map/all_to_all | solution.py:183
  471.6 62.9 %reduce-scatter.3.cloned.1.call-done = bf16[448,1024]{1,0:T(8,128)(2,1)} async-done(((bf16[1792,1024]{1,0:T(8,128)(2,1)}), bf16[448,1024]{1,0:T(8,128)(2,1)}) %reduce-scatter.3.cloned.1.call-update) | async-done | bytes 917520 | tf_op jit(solution)/shard_map/reduce_scatter | solution.py:176
  534.6 21.4 %all-to-all-done.1 = bf16[32,32,1792]{2,1,0:T(8,128)(2,1)} async-done(((bf16[32,32,1792]{2,1,0:T(8,128)(2,1)}), bf16[32,32,1792]{2,1,0:T(8,128)(2,1)}, u32[]{:S(2)}, u32[]{:S(2)}) %all-to-all-start.1) | async-done | bytes 3670048 | tf_op jit(solution)/shard_map/all_to_all | solution.py:183
  559.3 21.3 %reduce-scatter.5.cloned.1.call-done = bf16[56,1024]{1,0:T(8,128)(2,1)} async-done(((bf16[448,1024]{1,0:T(8,128)(2,1)}), bf16[56,1024]{1,0:T(8,128)(2,1)}) %reduce-scatter.5.cloned.1.call-update) | async-done | bytes 114704 | tf_op jit(solution)/shard_map/reduce_scatter | solution.py:177
  (222 shorter events, 106.9 us)
Async XLA Ops:
  10.4 11.8 %copy-start.7 = (bf16[1,56,1024]{2,1,0:T(8,128)(2,1)S(1)}, bf16[1,56,1024]{2,1,0:T(8,128)(2,1)}, u32[]{:S(2)}) copy-start(bf16[1,56,1024]{2,1,0:T(8,128)(2,1)} %param.17) | copy-start | bytes 344068
  10.4 117.5 %copy-start.4 = (f32[1,1792]{1,0:T(1,128)S(1)}, f32[1,1792]{1,0:T(1,128)}, u32[]{:S(2)}) copy-start(f32[1,1792]{1,0:T(1,128)} %param.19) | copy-start | bytes 21508
  10.4 162.6 %copy-start.2 = (bf16[2,1,64,1792]{3,2,1,0:T(8,128)(2,1)S(1)}, bf16[2,1,64,1792]{3,2,1,0:T(8,128)(2,1)}, u32[]{:S(2)}) copy-start(bf16[2,1,64,1792]{3,2,1,0:T(8,128)(2,1)} %param.15) | copy-start | bytes 1376260
  10.4 162.5 %all-to-all-start = ((bf16[32,32,1792]{2,1,0:T(8,128)(2,1)}), bf16[32,32,1792]{2,1,0:T(8,128)(2,1)}, u32[]{:S(2)}, u32[]{:S(2)}) async-start(bf16[32,32,1792]{2,1,0:T(8,128)(2,1)} %broadcast_in_dim.63), calls=%async_computation | async-start | bytes 7340032 | tf_op jit(solution)/shard_map/all_to_all | solution.py:171
  22.1 150.8 %all-gather.4.cloned.1.call-start = ((), (), s32[]{:S(2)}) async-start(), calls=%async_computation.6 | async-start | bytes 4587520 | tf_op jit(solution)/shard_map/all_gather | solution.py:165
  127.9 406.7 %reduce-scatter.3.cloned.1.call-start = ((), (), s32[]{:S(2)}) async-start(), calls=%async_computation.4 | async-start | bytes 4587520 | tf_op jit(solution)/shard_map/reduce_scatter | solution.py:176
  173.0 92.2 %copy-start.3 = (bf16[2,1,64,1792]{3,2,1,0:T(8,128)(2,1)S(1)}, bf16[2,1,64,1792]{3,2,1,0:T(8,128)(2,1)}, u32[]{:S(2)}) copy-start(bf16[2,1,64,1792]{3,2,1,0:T(8,128)(2,1)} %param.16) | copy-start | bytes 1376260
  173.9 7.3 %collective-permute-start = (bf16[64,1792]{1,0:T(8,128)(2,1)S(1)}, bf16[64,1792]{1,0:T(8,128)(2,1)S(1)}, u32[]{:S(2)}, u32[]{:S(2)}) collective-permute-start(bf16[64,1792]{1,0:T(8,128)(2,1)S(1)} %get-tuple-element.751), channel_id=1, source_target_pairs={{0,32},{32,64},{64,96},{96,128},{128,160},{160,192},{192,224},{1,3... | collective-permute-start | bytes 688136 | tf_op jit(solution)/shard_map/while/body/eval_jaxpr/ppermute | solution.py:11
  182.1 13.0 %collective-permute-start = (bf16[64,1792]{1,0:T(8,128)(2,1)S(1)}, bf16[64,1792]{1,0:T(8,128)(2,1)S(1)}, u32[]{:S(2)}, u32[]{:S(2)}) collective-permute-start(bf16[64,1792]{1,0:T(8,128)(2,1)S(1)} %get-tuple-element.751), channel_id=1, source_target_pairs={{0,32},{32,64},{64,96},{96,128},{128,160},{160,192},{192,224},{1,3... | collective-permute-start | bytes 688136 | tf_op jit(solution)/shard_map/while/body/eval_jaxpr/ppermute | solution.py:11
  201.8 7.3 %collective-permute-start = (bf16[64,1792]{1,0:T(8,128)(2,1)S(1)}, bf16[64,1792]{1,0:T(8,128)(2,1)S(1)}, u32[]{:S(2)}, u32[]{:S(2)}) collective-permute-start(bf16[64,1792]{1,0:T(8,128)(2,1)S(1)} %get-tuple-element.751), channel_id=1, source_target_pairs={{0,32},{32,64},{64,96},{96,128},{128,160},{160,192},{192,224},{1,3... | collective-permute-start | bytes 688136 | tf_op jit(solution)/shard_map/while/body/eval_jaxpr/ppermute | solution.py:11
  215.8 7.3 %collective-permute-start = (bf16[64,1792]{1,0:T(8,128)(2,1)S(1)}, bf16[64,1792]{1,0:T(8,128)(2,1)S(1)}, u32[]{:S(2)}, u32[]{:S(2)}) collective-permute-start(bf16[64,1792]{1,0:T(8,128)(2,1)S(1)} %get-tuple-element.751), channel_id=1, source_target_pairs={{0,32},{32,64},{64,96},{96,128},{128,160},{160,192},{192,224},{1,3... | collective-permute-start | bytes 688136 | tf_op jit(solution)/shard_map/while/body/eval_jaxpr/ppermute | solution.py:11
  224.0 7.3 %collective-permute-start = (bf16[64,1792]{1,0:T(8,128)(2,1)S(1)}, bf16[64,1792]{1,0:T(8,128)(2,1)S(1)}, u32[]{:S(2)}, u32[]{:S(2)}) collective-permute-start(bf16[64,1792]{1,0:T(8,128)(2,1)S(1)} %get-tuple-element.751), channel_id=1, source_target_pairs={{0,32},{32,64},{64,96},{96,128},{128,160},{160,192},{192,224},{1,3... | collective-permute-start | bytes 688136 | tf_op jit(solution)/shard_map/while/body/eval_jaxpr/ppermute | solution.py:11
  232.1 7.3 %collective-permute-start = (bf16[64,1792]{1,0:T(8,128)(2,1)S(1)}, bf16[64,1792]{1,0:T(8,128)(2,1)S(1)}, u32[]{:S(2)}, u32[]{:S(2)}) collective-permute-start(bf16[64,1792]{1,0:T(8,128)(2,1)S(1)} %get-tuple-element.751), channel_id=1, source_target_pairs={{0,32},{32,64},{64,96},{96,128},{128,160},{160,192},{192,224},{1,3... | collective-permute-start | bytes 688136 | tf_op jit(solution)/shard_map/while/body/eval_jaxpr/ppermute | solution.py:11
  240.3 8.4 %collective-permute-start = (bf16[64,1792]{1,0:T(8,128)(2,1)S(1)}, bf16[64,1792]{1,0:T(8,128)(2,1)S(1)}, u32[]{:S(2)}, u32[]{:S(2)}) collective-permute-start(bf16[64,1792]{1,0:T(8,128)(2,1)S(1)} %get-tuple-element.751), channel_id=1, source_target_pairs={{0,32},{32,64},{64,96},{96,128},{128,160},{160,192},{192,224},{1,3... | collective-permute-start | bytes 688136 | tf_op jit(solution)/shard_map/while/body/eval_jaxpr/ppermute | solution.py:11
  249.5 7.3 %collective-permute-start = (bf16[64,1792]{1,0:T(8,128)(2,1)S(1)}, bf16[64,1792]{1,0:T(8,128)(2,1)S(1)}, u32[]{:S(2)}, u32[]{:S(2)}) collective-permute-start(bf16[64,1792]{1,0:T(8,128)(2,1)S(1)} %get-tuple-element.751), channel_id=1, source_target_pairs={{0,32},{32,64},{64,96},{96,128},{128,160},{160,192},{192,224},{1,3... | collective-permute-start | bytes 688136 | tf_op jit(solution)/shard_map/while/body/eval_jaxpr/ppermute | solution.py:11
  257.6 7.3 %collective-permute-start = (bf16[64,1792]{1,0:T(8,128)(2,1)S(1)}, bf16[64,1792]{1,0:T(8,128)(2,1)S(1)}, u32[]{:S(2)}, u32[]{:S(2)}) collective-permute-start(bf16[64,1792]{1,0:T(8,128)(2,1)S(1)} %get-tuple-element.751), channel_id=1, source_target_pairs={{0,32},{32,64},{64,96},{96,128},{128,160},{160,192},{192,224},{1,3... | collective-permute-start | bytes 688136 | tf_op jit(solution)/shard_map/while/body/eval_jaxpr/ppermute | solution.py:11
  265.5 7.2 %collective-permute-start.1 = (bf16[64,1792]{1,0:T(8,128)(2,1)S(1)}, bf16[64,1792]{1,0:T(8,128)(2,1)S(1)}, u32[]{:S(2)}, u32[]{:S(2)}) collective-permute-start(bf16[64,1792]{1,0:T(8,128)(2,1)S(1)} %get-tuple-element.768), channel_id=1, source_target_pairs={{32,0},{64,32},{96,64},{128,96},{160,128},{192,160},{224,192},{33,... | collective-permute-start | bytes 688136 | tf_op jit(solution)/shard_map/while/body/eval_jaxpr/ppermute | solution.py:11
  272.9 9.1 %collective-permute-start.1 = (bf16[64,1792]{1,0:T(8,128)(2,1)S(1)}, bf16[64,1792]{1,0:T(8,128)(2,1)S(1)}, u32[]{:S(2)}, u32[]{:S(2)}) collective-permute-start(bf16[64,1792]{1,0:T(8,128)(2,1)S(1)} %get-tuple-element.768), channel_id=1, source_target_pairs={{32,0},{64,32},{96,64},{128,96},{160,128},{192,160},{224,192},{33,... | collective-permute-start | bytes 688136 | tf_op jit(solution)/shard_map/while/body/eval_jaxpr/ppermute | solution.py:11
  282.2 7.3 %collective-permute-start.1 = (bf16[64,1792]{1,0:T(8,128)(2,1)S(1)}, bf16[64,1792]{1,0:T(8,128)(2,1)S(1)}, u32[]{:S(2)}, u32[]{:S(2)}) collective-permute-start(bf16[64,1792]{1,0:T(8,128)(2,1)S(1)} %get-tuple-element.768), channel_id=1, source_target_pairs={{32,0},{64,32},{96,64},{128,96},{160,128},{192,160},{224,192},{33,... | collective-permute-start | bytes 688136 | tf_op jit(solution)/shard_map/while/body/eval_jaxpr/ppermute | solution.py:11
  289.8 8.0 %collective-permute-start.1 = (bf16[64,1792]{1,0:T(8,128)(2,1)S(1)}, bf16[64,1792]{1,0:T(8,128)(2,1)S(1)}, u32[]{:S(2)}, u32[]{:S(2)}) collective-permute-start(bf16[64,1792]{1,0:T(8,128)(2,1)S(1)} %get-tuple-element.768), channel_id=1, source_target_pairs={{32,0},{64,32},{96,64},{128,96},{160,128},{192,160},{224,192},{33,... | collective-permute-start | bytes 688136 | tf_op jit(solution)/shard_map/while/body/eval_jaxpr/ppermute | solution.py:11
  297.9 70.1 %collective-permute-start.1 = (bf16[64,1792]{1,0:T(8,128)(2,1)S(1)}, bf16[64,1792]{1,0:T(8,128)(2,1)S(1)}, u32[]{:S(2)}, u32[]{:S(2)}) collective-permute-start(bf16[64,1792]{1,0:T(8,128)(2,1)S(1)} %get-tuple-element.768), channel_id=1, source_target_pairs={{32,0},{64,32},{96,64},{128,96},{160,128},{192,160},{224,192},{33,... | collective-permute-start | bytes 688136 | tf_op jit(solution)/shard_map/while/body/eval_jaxpr/ppermute | solution.py:11
  371.6 6.5 %copy-start = (bf16[64,1024]{1,0:T(8,128)(2,1)}, bf16[64,1024]{1,0:T(8,128)(2,1)S(1)}, u32[]{:S(2)}) copy-start(bf16[64,1024]{1,0:T(8,128)(2,1)S(1)} %convolution_convert_fusion.1) | copy-start | bytes 393220 | tf_op jit(solution)/shard_map/while/body/eval_jaxpr/cond
  382.2 7.3 %collective-permute-start.1 = (bf16[64,1792]{1,0:T(8,128)(2,1)S(1)}, bf16[64,1792]{1,0:T(8,128)(2,1)S(1)}, u32[]{:S(2)}, u32[]{:S(2)}) collective-permute-start(bf16[64,1792]{1,0:T(8,128)(2,1)S(1)} %get-tuple-element.768), channel_id=1, source_target_pairs={{32,0},{64,32},{96,64},{128,96},{160,128},{192,160},{224,192},{33,... | collective-permute-start | bytes 688136 | tf_op jit(solution)/shard_map/while/body/eval_jaxpr/ppermute | solution.py:11
  393.1 6.5 %copy-start = (bf16[64,1024]{1,0:T(8,128)(2,1)}, bf16[64,1024]{1,0:T(8,128)(2,1)S(1)}, u32[]{:S(2)}) copy-start(bf16[64,1024]{1,0:T(8,128)(2,1)S(1)} %convolution_convert_fusion.1) | copy-start | bytes 393220 | tf_op jit(solution)/shard_map/while/body/eval_jaxpr/cond
  399.6 4.1 copy-start.1
  403.7 5.4 collective-permute-start.1
  409.3 21.3 %collective-permute-start.1 = (bf16[64,1792]{1,0:T(8,128)(2,1)S(1)}, bf16[64,1792]{1,0:T(8,128)(2,1)S(1)}, u32[]{:S(2)}, u32[]{:S(2)}) collective-permute-start(bf16[64,1792]{1,0:T(8,128)(2,1)S(1)} %get-tuple-element.768), channel_id=1, source_target_pairs={{32,0},{64,32},{96,64},{128,96},{160,128},{192,160},{224,192},{33,... | collective-permute-start | bytes 688136 | tf_op jit(solution)/shard_map/while/body/eval_jaxpr/ppermute | solution.py:11
  430.8 7.3 %collective-permute-start.1 = (bf16[64,1792]{1,0:T(8,128)(2,1)S(1)}, bf16[64,1792]{1,0:T(8,128)(2,1)S(1)}, u32[]{:S(2)}, u32[]{:S(2)}) collective-permute-start(bf16[64,1792]{1,0:T(8,128)(2,1)S(1)} %get-tuple-element.768), channel_id=1, source_target_pairs={{32,0},{64,32},{96,64},{128,96},{160,128},{192,160},{224,192},{33,... | collective-permute-start | bytes 688136 | tf_op jit(solution)/shard_map/while/body/eval_jaxpr/ppermute | solution.py:11
  462.6 93.4 %all-to-all-start.1 = ((bf16[32,32,1792]{2,1,0:T(8,128)(2,1)}), bf16[32,32,1792]{2,1,0:T(8,128)(2,1)}, u32[]{:S(2)}, u32[]{:S(2)}) async-start(bf16[32,32,1792]{2,1,0:T(8,128)(2,1)} %bitcast.99), calls=%async_computation.3 | async-start | bytes 7340032 | tf_op jit(solution)/shard_map/all_to_all | solution.py:183
  471.6 87.0 %copy-start.6 = (f32[1,32,1792]{2,1,0:T(8,128)S(1)}, f32[1,32,1792]{2,1,0:T(8,128)}, u32[]{:S(2)}) copy-start(f32[1,32,1792]{2,1,0:T(8,128)} %param.21) | copy-start | bytes 688132
  471.6 109.0 %copy-start.5 = (f32[1,56,1024]{2,1,0:T(8,128)S(1)}, f32[1,56,1024]{2,1,0:T(8,128)}, u32[]{:S(2)}) copy-start(f32[1,56,1024]{2,1,0:T(8,128)} %param.20) | copy-start | bytes 688132
  471.6 109.0 %reduce-scatter.5.cloned.1.call-start = ((), (), s32[]{:S(2)}) async-start(), calls=%async_computation.5 | async-start | bytes 1032192 | tf_op jit(solution)/shard_map/reduce_scatter | solution.py:177
  (1 other events, 4.1 us)
Sparse Core Ops, SparseCore 0:
  128.0 44.8 all-gather.3
  459.7 74.8 reduce-scatter.2
  537.1 43.4 reduce-scatter.4
where the time goes:
time: 590 us; the launch traced here: 589 us
  waiting for transfers between devices  283 us (48%)
  blocking collectives  124 us (21%)
  starting transfers between devices  89.1 us (15%)
  matrix products  43.4 us (7%)
  local copies, waits for them, and re-layouts  15 us (3%)
  between operations  13.9 us (2%)
  other arithmetic  10.6 us (2%)
  loops' own time  9.87 us (2%)
    ppermute x18, waiting for transfers between devices, from_behind(): return lax.ppermute(block, axis, route)  132 us
    all_gather x1, blocking collectives, gather_rows(): inner = lax.all_gather(shard, 'z', axis=0, tiled=True)  106 us
    ppermute x18, starting transfers between devices, from_behind(): return lax.ppermute(block, axis, route)  68.3 us
    reduce_scatter x1, waiting for transfers between devices, scatter_in_stages(): inner = lax.psum_scatter(block, 'y', scatter_dimension=0, tiled=True)  62.9 us
    all_gather x1, waiting for transfers between devices, gather_rows(): return lax.all_gather(inner, 'y', axis=0, tiled=True)  45 us
    all_to_all x1, waiting for transfers between devices, scatter_by_exchange(): arrived = lax.all_to_all(parts, DP, 0, 0, tiled=False)  21.4 us
    reduce_scatter x1, waiting for transfers between devices, scatter_in_stages(): lax.psum_scatter(inner, 'z', scatter_dimension=0, tiled=True)  21.3 us
    psum x1, blocking collectives, on_device(): total_squares = lax.psum(partial_squares, 'section')  18.2 us
  transfers between devices with their start and end apart: 23, of which 22 were waited for; matrix products, arithmetic and copies ran while one was open for 3% of the time, Pallas kernels for 0%

commit v1 on v0

--- a/solution.py
+++ b/solution.py
@@ -161,7 +161,9 @@
 
 
 def gather_rows(shard):
-    inner = lax.all_gather(shard, "z", axis=0, tiled=True)
+    inner = jnp.concatenate(
+        lax.all_to_all(jnp.stack([shard] * lax.axis_size("z")), "z", 0, 0), axis=0
+    )
     return lax.all_gather(inner, "y", axis=0, tiled=True)
 
 

time: 590 us -> 550 us (0.932)
  blocking collectives: 124 us -> 52.5 us
  waiting for transfers between devices: 283 us -> 323 us
  starting transfers between devices: 89.1 us -> 79.2 us
    all_gather x1 -> x0, blocking collectives: 106 us -> none  [gather_rows(): inner = lax.all_gather(shard, 'z', axis=0, tiled=True)]
    all_to_all x1, waiting for transfers between devices: 0.01 us -> 84.7 us  [exchange_rows(): parts = lax.all_to_all(copies, DP, 0, 0, tiled=False)]
    all_gather x1, waiting for transfers between devices: 45 us -> 0.01 us  [gather_rows(): return lax.all_gather(inner, 'y', axis=0, tiled=True)]
    all_to_all x0 -> x1, blocking collectives: none -> 34.3 us  [gather_rows(): lax.all_to_all(jnp.stack([shard] * lax.axis_size('z')), 'z', 0, 0)]
    all_to_all x1, starting transfers between devices: 11.7 us -> 5.1 us  [exchange_rows(): parts = lax.all_to_all(copies, DP, 0, 0, tiled=False)]
where the time goes in v1:
time: 550 us; the launch traced here: 549 us
  waiting for transfers between devices  323 us (59%)
  starting transfers between devices  79.2 us (14%)
  blocking collectives  52.5 us (10%)
  matrix products  43.4 us (8%)
  local copies, waits for them, and re-layouts  16 us (3%)
  between operations  13.9 us (3%)
  other arithmetic  10.6 us (2%)
  loops' own time  9.87 us (2%)
    ppermute x18, waiting for transfers between devices, from_behind(): return lax.ppermute(block, axis, route)  132 us
    all_to_all x1, waiting for transfers between devices, exchange_rows(): parts = lax.all_to_all(copies, DP, 0, 0, tiled=False)  84.7 us
    ppermute x18, starting transfers between devices, from_behind(): return lax.ppermute(block, axis, route)  68.3 us
    reduce_scatter x1, waiting for transfers between devices, scatter_in_stages(): inner = lax.psum_scatter(block, 'y', scatter_dimension=0, tiled=True)  62.9 us
    all_to_all x1, blocking collectives, gather_rows(): lax.all_to_all(jnp.stack([shard] * lax.axis_size('z')), 'z', 0, 0)  34.3 us
    all_to_all x1, waiting for transfers between devices, scatter_by_exchange(): arrived = lax.all_to_all(parts, DP, 0, 0, tiled=False)  21.4 us
    reduce_scatter x1, waiting for transfers between devices, scatter_in_stages(): lax.psum_scatter(inner, 'z', scatter_dimension=0, tiled=True)  21.3 us
    psum x1, blocking collectives, on_device(): total_squares = lax.psum(partial_squares, 'section')  18.2 us
  transfers between devices with their start and end apart: 23, of which 22 were waited for; matrix products, arithmetic and copies ran while one was open for 3% of the time, Pallas kernels for 0%

profile of v1, /device:TPU:2, one launch (start us, length us, event | category | flops | bytes accessed | tf_op | source)
XLA Modules:
  0.0 548.8 jit_solution(6434927749698815386)
XLA Ops:
  8.2 34.3 %all_to_all.15 = bf16[8,56,1024]{2,1,0:T(8,128)(2,1)} all-to-all(bf16[8,56,1024]{2,1,0:T(8,128)(2,1)S(1)} %stack.3), channel_id=1, replica_groups=mesh['section'=8,'y'=4,'z'=8] {'z'}, dimensions={0} | all-to-all | bytes 1835008 | tf_op jit(solution)/shard_map/all_to_all | solution.py:165
  45.7 5.1 all-to-all-start.1
  51.6 84.7 %all-to-all-done.1 = bf16[32,32,1792]{2,1,0:T(8,128)(2,1)} async-done(((bf16[32,32,1792]{2,1,0:T(8,128)(2,1)}), bf16[32,32,1792]{2,1,0:T(8,128)(2,1)}, u32[]{:S(2)}, u32[]{:S(2)}) %all-to-all-start.1) | async-done | bytes 3670048 | tf_op jit(solution)/shard_map/all_to_all | solution.py:173
  136.4 91.9 %while.39 = (s32[]{:T(128)}, bf16[64,1792]{1,0:T(8,128)(2,1)S(1)}, bf16[2,64,1792]{2,1,0:T(8,128)(2,1)S(1)}, bf16[2,64,1024]{2,1,0:T(8,128)(2,1)S(1)}, s32[]{:T(...) while((s32[]{:T(128)}, bf16[64,1792]{1,0:T(8,128)(2,1)S(1)}, ...), condition=%wide.region_4.5_spmd, body=%wide.region_0.4_spmd.sunk | while | flops 471269440 | bytes 11721002 | solution.py:91
  139.3 5.3 collective-permute-done
  147.4 10.9 %collective-permute-done = bf16[64,1792]{1,0:T(8,128)(2,1)S(1)} collective-permute-done((bf16[64,1792]{1,0:T(8,128)(2,1)S(1)}, bf16[64,1792]{1,0:T(8,128)(2,1)S(1)}, u32[]{:S(2)}, u32[]{:S(2)}) %collective-permute-start) | collective-permute-done | bytes 229408 | tf_op jit(solution)/shard_map/while/body/eval_jaxpr/ppermute | solution.py:11
  158.5 6.6 %conditional.4 = (bf16[64,1024]{1,0:T(8,128)(2,1)}, bf16[64,1792]{1,0:T(8,128)(2,1)S(1)}) conditional(s32[]{:T(128)} %convert_element_type.145, () %tuple.96, (bf16[64,1792]{1,0:T(8,128)(2,1)S(1)}, f32[1,1792]{1,0:T(1,128)S(1)}, bf16[1792,1024]{1,0:T(8,128)(2,1)}, bf16[1024,1792]{1,0:T(8,128)(2,1)}) %tuple.97), branch_computations={%region_1.1_spmd, %region_2.3_spmd} | conditional | flops 470974528 | bytes 8542228 | solution.py:74
  168.0 4.4 collective-permute-done
  172.5 6.6 %conditional.4 = (bf16[64,1024]{1,0:T(8,128)(2,1)}, bf16[64,1792]{1,0:T(8,128)(2,1)S(1)}) conditional(s32[]{:T(128)} %convert_element_type.145, () %tuple.96, (bf16[64,1792]{1,0:T(8,128)(2,1)S(1)}, f32[1,1792]{1,0:T(1,128)S(1)}, bf16[1792,1024]{1,0:T(8,128)(2,1)}, bf16[1024,1792]{1,0:T(8,128)(2,1)}) %tuple.97), branch_computations={%region_1.1_spmd, %region_2.3_spmd} | conditional | flops 470974528 | bytes 8542228 | solution.py:74
  172.8 3.5 convolution_convert_fusion
  182.0 4.4 collective-permute-done
  187.3 3.8 collective-permute-start
  197.5 5.3 collective-permute-done
  203.6 7.3 %collective-permute-start = (bf16[64,1792]{1,0:T(8,128)(2,1)S(1)}, bf16[64,1792]{1,0:T(8,128)(2,1)S(1)}, u32[]{:S(2)}, u32[]{:S(2)}) collective-permute-start(bf16[64,1792]{1,0:T(8,128)(2,1)S(1)} %get-tuple-element.751), channel_id=1, source_target_pairs={{0,32},{32,64},{64,96},{96,128},{128,160},{160,192},{192,224},{1,3... | collective-permute-start | bytes 688136 | tf_op jit(solution)/shard_map/while/body/eval_jaxpr/ppermute | solution.py:11
  212.8 6.2 %collective-permute-start = (bf16[64,1792]{1,0:T(8,128)(2,1)S(1)}, bf16[64,1792]{1,0:T(8,128)(2,1)S(1)}, u32[]{:S(2)}, u32[]{:S(2)}) collective-permute-start(bf16[64,1792]{1,0:T(8,128)(2,1)S(1)} %get-tuple-element.751), channel_id=1, source_target_pairs={{0,32},{32,64},{64,96},{96,128},{128,160},{160,192},{192,224},{1,3... | collective-permute-start | bytes 688136 | tf_op jit(solution)/shard_map/while/body/eval_jaxpr/ppermute | solution.py:11
  221.0 6.2 %collective-permute-start = (bf16[64,1792]{1,0:T(8,128)(2,1)S(1)}, bf16[64,1792]{1,0:T(8,128)(2,1)S(1)}, u32[]{:S(2)}, u32[]{:S(2)}) collective-permute-start(bf16[64,1792]{1,0:T(8,128)(2,1)S(1)} %get-tuple-element.751), channel_id=1, source_target_pairs={{0,32},{32,64},{64,96},{96,128},{128,160},{160,192},{192,224},{1,3... | collective-permute-start | bytes 688136 | tf_op jit(solution)/shard_map/while/body/eval_jaxpr/ppermute | solution.py:11
  228.6 172.9 %while.40 = (s32[]{:T(128)}, bf16[64,1792]{1,0:T(8,128)(2,1)S(1)}, bf16[2,64,1792]{2,1,0:T(8,128)(2,1)S(1)}, bf16[2,64,1024]{2,1,0:T(8,128)(2,1)S(1)}, f32[2,1]{...) while((s32[]{:T(128)}, bf16[64,1792]{1,0:T(8,128)(2,1)S(1)}, ...), condition=%wide.region_13.14_spmd, body=%wide.region_6.0_spmd.sunk | while | flops 949518400 | bytes 14876903 | solution.py:156
  232.1 3.9 collective-permute-done.1
  239.7 5.7 %collective-permute-done.1 = bf16[64,1792]{1,0:T(8,128)(2,1)S(1)} collective-permute-done((bf16[64,1792]{1,0:T(8,128)(2,1)S(1)}, bf16[64,1792]{1,0:T(8,128)(2,1)S(1)}, u32[]{:S(2)}, u32[]{:S(2)}) %collective-permute-start.1) | collective-permute-done | bytes 229408 | tf_op jit(solution)/shard_map/while/body/eval_jaxpr/ppermute | solution.py:11
  248.8 4.1 collective-permute-done.1
  256.4 4.7 collective-permute-done.1
  264.5 66.8 %collective-permute-done.1 = bf16[64,1792]{1,0:T(8,128)(2,1)S(1)} collective-permute-done((bf16[64,1792]{1,0:T(8,128)(2,1)S(1)}, bf16[64,1792]{1,0:T(8,128)(2,1)S(1)}, u32[]{:S(2)}, u32[]{:S(2)}) %collective-permute-start.1) | collective-permute-done | bytes 229408 | tf_op jit(solution)/shard_map/while/body/eval_jaxpr/ppermute | solution.py:11
  331.5 14.0 %conditional.5 = (bf16[64,1792]{1,0:T(8,128)(2,1)S(1)}, bf16[64,1024]{1,0:T(8,128)(2,1)S(1)}, f32[1]{0:T(128)}) conditional(s32[]{:T(128)} %convert_element_type.146, () %tuple.100, (bf16[64,1792]{1,0:T(8,128)(2,1)S(1)}, bf16[2,64,1792]{2,1,0:T(8,128)(2,1)S(1)}, s32[]{:T(128)}, bf16[1024,1792]{1,0:T(8,128)(2,1)}, bf16[1792,1024]{1,0:T(8,128)(2,1)}, ...), branch_computations={%region_7.7_spmd, %region_8.12_spmd} | conditional | flops 949223488 | bytes 11698044 | solution.py:132
  348.8 4.1 collective-permute-done.1
  353.0 14.0 %conditional.5 = (bf16[64,1792]{1,0:T(8,128)(2,1)S(1)}, bf16[64,1024]{1,0:T(8,128)(2,1)S(1)}, f32[1]{0:T(128)}) conditional(s32[]{:T(128)} %convert_element_type.146, () %tuple.100, (bf16[64,1792]{1,0:T(8,128)(2,1)S(1)}, bf16[2,64,1792]{2,1,0:T(8,128)(2,1)S(1)}, s32[]{:T(128)}, bf16[1024,1792]{1,0:T(8,128)(2,1)}, bf16[1792,1024]{1,0:T(8,128)(2,1)}, ...), branch_computations={%region_7.7_spmd, %region_8.12_spmd} | conditional | flops 949223488 | bytes 11698044 | solution.py:132
  372.7 17.8 %collective-permute-start.1 = (bf16[64,1792]{1,0:T(8,128)(2,1)S(1)}, bf16[64,1792]{1,0:T(8,128)(2,1)S(1)}, u32[]{:S(2)}, u32[]{:S(2)}) collective-permute-start(bf16[64,1792]{1,0:T(8,128)(2,1)S(1)} %get-tuple-element.768), channel_id=1, source_target_pairs={{32,0},{64,32},{96,64},{128,96},{160,128},{192,160},{224,192},{33,... | collective-permute-start | bytes 688136 | tf_op jit(solution)/shard_map/while/body/eval_jaxpr/ppermute | solution.py:11
  394.2 3.8 collective-permute-start.1
  401.5 18.2 %psum.7 = f32[2,1]{0,1:T(1,128)S(1)} all-reduce(f32[2,1]{0,1:T(1,128)S(1)} %get-tuple-element.560), channel_id=1, replica_groups=mesh['section'=8,'y'=4,'z'=8] {'section'}, use_global_device_ids=true, to_apply=%region_14.15 | all-reduce | flops 2 | bytes 16 | tf_op jit(solution)/shard_map/psum | solution.py:201
  426.0 5.7 %all-to-all-start.2 = ((bf16[32,32,1792]{2,1,0:T(8,128)(2,1)}), bf16[32,32,1792]{2,1,0:T(8,128)(2,1)}, u32[]{:S(2)}, u32[]{:S(2)}) async-start(bf16[32,32,1792]{2,1,0:T(8,128)(2,1)} %bitcast.99), calls=%async_computation.4 | async-start | bytes 7340032 | tf_op jit(solution)/shard_map/all_to_all | solution.py:185
  431.7 62.9 %reduce-scatter.3.cloned.1.call-done = bf16[448,1024]{1,0:T(8,128)(2,1)} async-done(((bf16[1792,1024]{1,0:T(8,128)(2,1)}), bf16[448,1024]{1,0:T(8,128)(2,1)}) %reduce-scatter.3.cloned.1.call-update) | async-done | bytes 917520 | tf_op jit(solution)/shard_map/reduce_scatter | solution.py:178
  494.7 21.4 %all-to-all-done.2 = bf16[32,32,1792]{2,1,0:T(8,128)(2,1)} async-done(((bf16[32,32,1792]{2,1,0:T(8,128)(2,1)}), bf16[32,32,1792]{2,1,0:T(8,128)(2,1)}, u32[]{:S(2)}, u32[]{:S(2)}) %all-to-all-start.2) | async-done | bytes 3670048 | tf_op jit(solution)/shard_map/all_to_all | solution.py:185
  519.4 21.3 %reduce-scatter.5.cloned.1.call-done = bf16[56,1024]{1,0:T(8,128)(2,1)} async-done(((bf16[448,1024]{1,0:T(8,128)(2,1)}), bf16[56,1024]{1,0:T(8,128)(2,1)}) %reduce-scatter.5.cloned.1.call-update) | async-done | bytes 114704 | tf_op jit(solution)/shard_map/reduce_scatter | solution.py:179
  (221 shorter events, 108.6 us)
Async XLA Ops:
  45.7 5.9 %copy-start.4 = (f32[1,1792]{1,0:T(1,128)S(1)}, f32[1,1792]{1,0:T(1,128)}, u32[]{:S(2)}) copy-start(f32[1,1792]{1,0:T(1,128)} %param.19) | copy-start | bytes 21508
  45.7 90.7 %copy-start.2 = (bf16[2,1,64,1792]{3,2,1,0:T(8,128)(2,1)S(1)}, bf16[2,1,64,1792]{3,2,1,0:T(8,128)(2,1)}, u32[]{:S(2)}) copy-start(bf16[2,1,64,1792]{3,2,1,0:T(8,128)(2,1)} %param.15) | copy-start | bytes 1376260
  45.7 90.6 %all-to-all-start.1 = ((bf16[32,32,1792]{2,1,0:T(8,128)(2,1)}), bf16[32,32,1792]{2,1,0:T(8,128)(2,1)}, u32[]{:S(2)}, u32[]{:S(2)}) async-start(bf16[32,32,1792]{2,1,0:T(8,128)(2,1)} %broadcast_in_dim.63), calls=%async_computation.1 | async-start | bytes 7340032 | tf_op jit(solution)/shard_map/all_to_all | solution.py:173
  50.8 85.5 %all-gather.2.cloned.1.call-start = ((), (), s32[]{:S(2)}) async-start(), calls=%async_computation.5 | async-start | bytes 4587520 | tf_op jit(solution)/shard_map/all_gather | solution.py:167
  51.5 443.1 %reduce-scatter.3.cloned.1.call-start = ((), (), s32[]{:S(2)}) async-start(), calls=%async_computation.6 | async-start | bytes 4587520 | tf_op jit(solution)/shard_map/reduce_scatter | solution.py:178
  136.4 92.2 %copy-start.3 = (bf16[2,1,64,1792]{3,2,1,0:T(8,128)(2,1)S(1)}, bf16[2,1,64,1792]{3,2,1,0:T(8,128)(2,1)}, u32[]{:S(2)}) copy-start(bf16[2,1,64,1792]{3,2,1,0:T(8,128)(2,1)} %param.16) | copy-start | bytes 1376260
  137.3 7.3 %collective-permute-start = (bf16[64,1792]{1,0:T(8,128)(2,1)S(1)}, bf16[64,1792]{1,0:T(8,128)(2,1)S(1)}, u32[]{:S(2)}, u32[]{:S(2)}) collective-permute-start(bf16[64,1792]{1,0:T(8,128)(2,1)S(1)} %get-tuple-element.751), channel_id=1, source_target_pairs={{0,32},{32,64},{64,96},{96,128},{128,160},{160,192},{192,224},{1,3... | collective-permute-start | bytes 688136 | tf_op jit(solution)/shard_map/while/body/eval_jaxpr/ppermute | solution.py:11
  145.4 12.9 %collective-permute-start = (bf16[64,1792]{1,0:T(8,128)(2,1)S(1)}, bf16[64,1792]{1,0:T(8,128)(2,1)S(1)}, u32[]{:S(2)}, u32[]{:S(2)}) collective-permute-start(bf16[64,1792]{1,0:T(8,128)(2,1)S(1)} %get-tuple-element.751), channel_id=1, source_target_pairs={{0,32},{32,64},{64,96},{96,128},{128,160},{160,192},{192,224},{1,3... | collective-permute-start | bytes 688136 | tf_op jit(solution)/shard_map/while/body/eval_jaxpr/ppermute | solution.py:11
  165.1 7.3 %collective-permute-start = (bf16[64,1792]{1,0:T(8,128)(2,1)S(1)}, bf16[64,1792]{1,0:T(8,128)(2,1)S(1)}, u32[]{:S(2)}, u32[]{:S(2)}) collective-permute-start(bf16[64,1792]{1,0:T(8,128)(2,1)S(1)} %get-tuple-element.751), channel_id=1, source_target_pairs={{0,32},{32,64},{64,96},{96,128},{128,160},{160,192},{192,224},{1,3... | collective-permute-start | bytes 688136 | tf_op jit(solution)/shard_map/while/body/eval_jaxpr/ppermute | solution.py:11
  179.1 7.3 %collective-permute-start = (bf16[64,1792]{1,0:T(8,128)(2,1)S(1)}, bf16[64,1792]{1,0:T(8,128)(2,1)S(1)}, u32[]{:S(2)}, u32[]{:S(2)}) collective-permute-start(bf16[64,1792]{1,0:T(8,128)(2,1)S(1)} %get-tuple-element.751), channel_id=1, source_target_pairs={{0,32},{32,64},{64,96},{96,128},{128,160},{160,192},{192,224},{1,3... | collective-permute-start | bytes 688136 | tf_op jit(solution)/shard_map/while/body/eval_jaxpr/ppermute | solution.py:11
  187.3 7.3 %collective-permute-start = (bf16[64,1792]{1,0:T(8,128)(2,1)S(1)}, bf16[64,1792]{1,0:T(8,128)(2,1)S(1)}, u32[]{:S(2)}, u32[]{:S(2)}) collective-permute-start(bf16[64,1792]{1,0:T(8,128)(2,1)S(1)} %get-tuple-element.751), channel_id=1, source_target_pairs={{0,32},{32,64},{64,96},{96,128},{128,160},{160,192},{192,224},{1,3... | collective-permute-start | bytes 688136 | tf_op jit(solution)/shard_map/while/body/eval_jaxpr/ppermute | solution.py:11
  195.5 7.3 %collective-permute-start = (bf16[64,1792]{1,0:T(8,128)(2,1)S(1)}, bf16[64,1792]{1,0:T(8,128)(2,1)S(1)}, u32[]{:S(2)}, u32[]{:S(2)}) collective-permute-start(bf16[64,1792]{1,0:T(8,128)(2,1)S(1)} %get-tuple-element.751), channel_id=1, source_target_pairs={{0,32},{32,64},{64,96},{96,128},{128,160},{160,192},{192,224},{1,3... | collective-permute-start | bytes 688136 | tf_op jit(solution)/shard_map/while/body/eval_jaxpr/ppermute | solution.py:11
  203.6 8.4 %collective-permute-start = (bf16[64,1792]{1,0:T(8,128)(2,1)S(1)}, bf16[64,1792]{1,0:T(8,128)(2,1)S(1)}, u32[]{:S(2)}, u32[]{:S(2)}) collective-permute-start(bf16[64,1792]{1,0:T(8,128)(2,1)S(1)} %get-tuple-element.751), channel_id=1, source_target_pairs={{0,32},{32,64},{64,96},{96,128},{128,160},{160,192},{192,224},{1,3... | collective-permute-start | bytes 688136 | tf_op jit(solution)/shard_map/while/body/eval_jaxpr/ppermute | solution.py:11
  212.8 7.3 %collective-permute-start = (bf16[64,1792]{1,0:T(8,128)(2,1)S(1)}, bf16[64,1792]{1,0:T(8,128)(2,1)S(1)}, u32[]{:S(2)}, u32[]{:S(2)}) collective-permute-start(bf16[64,1792]{1,0:T(8,128)(2,1)S(1)} %get-tuple-element.751), channel_id=1, source_target_pairs={{0,32},{32,64},{64,96},{96,128},{128,160},{160,192},{192,224},{1,3... | collective-permute-start | bytes 688136 | tf_op jit(solution)/shard_map/while/body/eval_jaxpr/ppermute | solution.py:11
  221.0 7.3 %collective-permute-start = (bf16[64,1792]{1,0:T(8,128)(2,1)S(1)}, bf16[64,1792]{1,0:T(8,128)(2,1)S(1)}, u32[]{:S(2)}, u32[]{:S(2)}) collective-permute-start(bf16[64,1792]{1,0:T(8,128)(2,1)S(1)} %get-tuple-element.751), channel_id=1, source_target_pairs={{0,32},{32,64},{64,96},{96,128},{128,160},{160,192},{192,224},{1,3... | collective-permute-start | bytes 688136 | tf_op jit(solution)/shard_map/while/body/eval_jaxpr/ppermute | solution.py:11
  228.8 7.2 %collective-permute-start.1 = (bf16[64,1792]{1,0:T(8,128)(2,1)S(1)}, bf16[64,1792]{1,0:T(8,128)(2,1)S(1)}, u32[]{:S(2)}, u32[]{:S(2)}) collective-permute-start(bf16[64,1792]{1,0:T(8,128)(2,1)S(1)} %get-tuple-element.768), channel_id=1, source_target_pairs={{32,0},{64,32},{96,64},{128,96},{160,128},{192,160},{224,192},{33,... | collective-permute-start | bytes 688136 | tf_op jit(solution)/shard_map/while/body/eval_jaxpr/ppermute | solution.py:11
  236.2 9.1 %collective-permute-start.1 = (bf16[64,1792]{1,0:T(8,128)(2,1)S(1)}, bf16[64,1792]{1,0:T(8,128)(2,1)S(1)}, u32[]{:S(2)}, u32[]{:S(2)}) collective-permute-start(bf16[64,1792]{1,0:T(8,128)(2,1)S(1)} %get-tuple-element.768), channel_id=1, source_target_pairs={{32,0},{64,32},{96,64},{128,96},{160,128},{192,160},{224,192},{33,... | collective-permute-start | bytes 688136 | tf_op jit(solution)/shard_map/while/body/eval_jaxpr/ppermute | solution.py:11
  245.6 7.3 %collective-permute-start.1 = (bf16[64,1792]{1,0:T(8,128)(2,1)S(1)}, bf16[64,1792]{1,0:T(8,128)(2,1)S(1)}, u32[]{:S(2)}, u32[]{:S(2)}) collective-permute-start(bf16[64,1792]{1,0:T(8,128)(2,1)S(1)} %get-tuple-element.768), channel_id=1, source_target_pairs={{32,0},{64,32},{96,64},{128,96},{160,128},{192,160},{224,192},{33,... | collective-permute-start | bytes 688136 | tf_op jit(solution)/shard_map/while/body/eval_jaxpr/ppermute | solution.py:11
  253.1 8.0 %collective-permute-start.1 = (bf16[64,1792]{1,0:T(8,128)(2,1)S(1)}, bf16[64,1792]{1,0:T(8,128)(2,1)S(1)}, u32[]{:S(2)}, u32[]{:S(2)}) collective-permute-start(bf16[64,1792]{1,0:T(8,128)(2,1)S(1)} %get-tuple-element.768), channel_id=1, source_target_pairs={{32,0},{64,32},{96,64},{128,96},{160,128},{192,160},{224,192},{33,... | collective-permute-start | bytes 688136 | tf_op jit(solution)/shard_map/while/body/eval_jaxpr/ppermute | solution.py:11
  261.3 70.1 %collective-permute-start.1 = (bf16[64,1792]{1,0:T(8,128)(2,1)S(1)}, bf16[64,1792]{1,0:T(8,128)(2,1)S(1)}, u32[]{:S(2)}, u32[]{:S(2)}) collective-permute-start(bf16[64,1792]{1,0:T(8,128)(2,1)S(1)} %get-tuple-element.768), channel_id=1, source_target_pairs={{32,0},{64,32},{96,64},{128,96},{160,128},{192,160},{224,192},{33,... | collective-permute-start | bytes 688136 | tf_op jit(solution)/shard_map/while/body/eval_jaxpr/ppermute | solution.py:11
  334.9 6.5 %copy-start = (bf16[64,1024]{1,0:T(8,128)(2,1)}, bf16[64,1024]{1,0:T(8,128)(2,1)S(1)}, u32[]{:S(2)}) copy-start(bf16[64,1024]{1,0:T(8,128)(2,1)S(1)} %convolution_convert_fusion.1) | copy-start | bytes 393220 | tf_op jit(solution)/shard_map/while/body/eval_jaxpr/cond
  341.4 4.1 copy-start.1
  345.5 7.3 %collective-permute-start.1 = (bf16[64,1792]{1,0:T(8,128)(2,1)S(1)}, bf16[64,1792]{1,0:T(8,128)(2,1)S(1)}, u32[]{:S(2)}, u32[]{:S(2)}) collective-permute-start(bf16[64,1792]{1,0:T(8,128)(2,1)S(1)} %get-tuple-element.768), channel_id=1, source_target_pairs={{32,0},{64,32},{96,64},{128,96},{160,128},{192,160},{224,192},{33,... | collective-permute-start | bytes 688136 | tf_op jit(solution)/shard_map/while/body/eval_jaxpr/ppermute | solution.py:11
  356.4 6.5 %copy-start = (bf16[64,1024]{1,0:T(8,128)(2,1)}, bf16[64,1024]{1,0:T(8,128)(2,1)S(1)}, u32[]{:S(2)}) copy-start(bf16[64,1024]{1,0:T(8,128)(2,1)S(1)} %convolution_convert_fusion.1) | copy-start | bytes 393220 | tf_op jit(solution)/shard_map/while/body/eval_jaxpr/cond
  362.9 4.1 copy-start.1
  367.0 5.4 collective-permute-start.1
  372.7 21.3 %collective-permute-start.1 = (bf16[64,1792]{1,0:T(8,128)(2,1)S(1)}, bf16[64,1792]{1,0:T(8,128)(2,1)S(1)}, u32[]{:S(2)}, u32[]{:S(2)}) collective-permute-start(bf16[64,1792]{1,0:T(8,128)(2,1)S(1)} %get-tuple-element.768), channel_id=1, source_target_pairs={{32,0},{64,32},{96,64},{128,96},{160,128},{192,160},{224,192},{33,... | collective-permute-start | bytes 688136 | tf_op jit(solution)/shard_map/while/body/eval_jaxpr/ppermute | solution.py:11
  394.2 7.3 %collective-permute-start.1 = (bf16[64,1792]{1,0:T(8,128)(2,1)S(1)}, bf16[64,1792]{1,0:T(8,128)(2,1)S(1)}, u32[]{:S(2)}, u32[]{:S(2)}) collective-permute-start(bf16[64,1792]{1,0:T(8,128)(2,1)S(1)} %get-tuple-element.768), channel_id=1, source_target_pairs={{32,0},{64,32},{96,64},{128,96},{160,128},{192,160},{224,192},{33,... | collective-permute-start | bytes 688136 | tf_op jit(solution)/shard_map/while/body/eval_jaxpr/ppermute | solution.py:11
  426.0 90.1 %all-to-all-start.2 = ((bf16[32,32,1792]{2,1,0:T(8,128)(2,1)}), bf16[32,32,1792]{2,1,0:T(8,128)(2,1)}, u32[]{:S(2)}, u32[]{:S(2)}) async-start(bf16[32,32,1792]{2,1,0:T(8,128)(2,1)} %bitcast.99), calls=%async_computation.4 | async-start | bytes 7340032 | tf_op jit(solution)/shard_map/all_to_all | solution.py:185
  431.7 87.0 %copy-start.6 = (f32[1,32,1792]{2,1,0:T(8,128)S(1)}, f32[1,32,1792]{2,1,0:T(8,128)}, u32[]{:S(2)}) copy-start(f32[1,32,1792]{2,1,0:T(8,128)} %param.21) | copy-start | bytes 688132
  431.7 109.0 %copy-start.5 = (f32[1,56,1024]{2,1,0:T(8,128)S(1)}, f32[1,56,1024]{2,1,0:T(8,128)}, u32[]{:S(2)}) copy-start(f32[1,56,1024]{2,1,0:T(8,128)} %param.20) | copy-start | bytes 688132
  431.7 109.0 %reduce-scatter.5.cloned.1.call-start = ((), (), s32[]{:S(2)}) async-start(), calls=%async_computation.7 | async-start | bytes 1032192 | tf_op jit(solution)/shard_map/reduce_scatter | solution.py:179
Sparse Core Ops, SparseCore 0:
  53.5 74.0 all-gather.1
  423.0 71.6 reduce-scatter.2
  497.2 43.3 reduce-scatter.4
